TPU v7x, 32 devices: a whole 2x2x4 slice. The times are simulated.
32 devices in a mesh: chan: 4 (over y, x), hid: 8 (over z, core).
Axes of the slice: x: 2, y: 2, z: 4, core: 2. Of those that a mesh axis runs over, the one named last changes fastest.
Arguments:
- pixels: bfloat16 [384, 256, 256], P('chan'), may hold values from -6 to 6
- patch_weight: bfloat16 [384, 256, 6144], P('chan', None, 'hid'), may hold values from -0.375 to 0.375
- channel_embed: bfloat16 [384, 6144], P('chan', 'hid'), may hold values from -3 to 3
- pool_query: bfloat16 [48, 6144], P('chan', 'hid'), may hold values from -2.5 to 2.5
- group_mix: bfloat16 [48, 6144], P('chan', 'hid'), may hold values from -3.2 to 3.2
- assign: int32 [384], P('chan'), may hold values from 0 to 47, as said below
- ln_gain: float32 [6144], P('chan'), may hold values from 0.1 to 1.9
- w_qkv: bfloat16 [6144, 3, 6144], P('chan', None, 'hid'), may hold values from -0.078125 to 0.078125
- w_up: bfloat16 [6144, 24576], P('chan', 'hid'), may hold values from -0.078125 to 0.078125
- b_up: float32 [24576], P('hid'), may hold values from -3 to 3
- w_out: bfloat16 [6144, 6144], P('hid', 'chan'), may hold values from -0.078125 to 0.078125
- w_down: bfloat16 [24576, 6144], P('hid', 'chan'), may hold values from -0.0390625 to 0.0390625
Outputs:
- block_out: bfloat16 [256, 6144], P(None, 'chan')
Inputs may be any that keep to these rules, and one draw needn't show every extreme that they name: Channel c belongs to group assign[c]; every group holds exactly 8 channels, and group k's channels all lie among the 96 consecutive channels beginning at channel (k // 12) * 96.
All inputs are finite; a program needn't handle non-finite values.
Results may differ from a plain program's by a relative error of at most 0.02.
Values may be sent and summed in bfloat16 or wider, within the bound.
A program may use at most 320 MiB of HBM per device.

v0:
```python
import math
import jax
import jax.numpy as jnp
from jax import lax
from jax.sharding import PartitionSpec as P

HS = 128
PATCHES = 256
D = 6144
epsilon = 1e-06


def head_norm(values):
    return values * lax.rsqrt(jnp.mean(values * values, axis=-1, keepdims=True) + epsilon)


def finish_rows(qkv_rows, up_rows, b_up, heads_dev):
    rows = qkv_rows.shape[0]
    width = heads_dev * HS
    query_part = (
        head_norm(qkv_rows[:, 0].reshape(rows, heads_dev, HS))
        .astype(jnp.bfloat16)
        .reshape(rows, width)
    )
    key_part = (
        head_norm(qkv_rows[:, 1].reshape(rows, heads_dev, HS))
        .astype(jnp.bfloat16)
        .reshape(rows, width)
    )
    value_part = qkv_rows[:, 2].astype(jnp.bfloat16)
    hidden_part = jax.nn.gelu(up_rows + b_up, approximate=False).astype(jnp.bfloat16)
    return (query_part, key_part, value_part, hidden_part)


def on_device(
    pixels,
    patch_weight,
    channel_embed,
    pool_query,
    group_mix,
    assign,
    ln_gain,
    w_qkv,
    w_up,
    b_up,
    w_out,
    w_down,
):
    chan_count = pixels.shape[0]
    tok_count = pixels.shape[1]
    width_hid = patch_weight.shape[2]
    width_chan = ln_gain.shape[0]
    heads_dev = width_hid // HS
    groups_dev = pool_query.shape[0]
    embedded = jnp.einsum("ctp,cpd->ctd", pixels, patch_weight, preferred_element_type=jnp.float32)
    embedded = embedded + channel_embed.astype(jnp.float32)[:, None, :]
    features = jax.nn.gelu(embedded, approximate=False)
    split = features.reshape(chan_count, tok_count, heads_dev, HS)
    normed = head_norm(split)
    local_group = assign - lax.axis_index("chan") * groups_dev
    member = (local_group[None, :] == jnp.arange(groups_dev, dtype=jnp.int32)[:, None]).astype(
        jnp.float32
    )
    query = jnp.dot(member.T, pool_query.astype(jnp.float32), precision=lax.Precision.HIGHEST)
    query = query.reshape(chan_count, heads_dev, HS)
    score = jnp.einsum("cthe,che->cth", normed, query, precision=lax.Precision.HIGHEST) / math.sqrt(
        HS
    )
    shift = jnp.sqrt(jnp.sum(query * query, axis=-1))
    weight = jnp.exp(score - shift[:, None, :])
    numer = jnp.einsum(
        "kc,cthe->kthe", member, weight[..., None] * split, precision=lax.Precision.HIGHEST
    )
    denom = jnp.einsum("kc,cth->kth", member, weight, precision=lax.Precision.HIGHEST)
    pooled = (numer / denom[..., None]).reshape(groups_dev, tok_count, width_hid)
    partial_value = jnp.einsum(
        "kd,ktd->td", group_mix.astype(jnp.float32), pooled, precision=lax.Precision.HIGHEST
    )
    layer_sum = lax.psum(partial_value.astype(jnp.bfloat16), "chan")
    gathered = lax.all_gather(layer_sum, "hid", axis=1, tiled=True)
    wide = gathered.astype(jnp.float32)
    row_total = jnp.sum(wide, axis=1)
    row_square = jnp.sum(wide * wide, axis=1)
    mine = lax.dynamic_slice_in_dim(gathered, lax.axis_index("chan") * width_chan, width_chan, 1)
    row_mean = row_total / D
    row_var = row_square / D - row_mean * row_mean
    own_cols = mine.astype(jnp.float32)
    normed_input = (
        (own_cols - row_mean[:, None]) * lax.rsqrt(row_var + epsilon)[:, None] * ln_gain
    ).astype(jnp.bfloat16)
    qkv_part = jnp.einsum("td,dke->tke", normed_input, w_qkv, preferred_element_type=jnp.float32)
    up_part = jnp.dot(normed_input, w_up, preferred_element_type=jnp.float32)
    qkv_share, up_share = (
        lax.psum_scatter(
            qkv_part.astype(jnp.bfloat16), "chan", scatter_dimension=0, tiled=True
        ).astype(jnp.float32),
        lax.psum_scatter(
            up_part.astype(jnp.bfloat16), "chan", scatter_dimension=0, tiled=True
        ).astype(jnp.float32),
    )
    query_share, key_share, value_share, hidden_share = finish_rows(
        qkv_share, up_share, b_up, heads_dev
    )
    query_rows, key_rows, value_rows, hidden = (
        lax.all_gather(query_share, "chan", axis=0, tiled=True),
        lax.all_gather(key_share, "chan", axis=0, tiled=True),
        lax.all_gather(value_share, "chan", axis=0, tiled=True),
        lax.all_gather(hidden_share, "chan", axis=0, tiled=True),
    )
    images = tok_count // PATCHES
    queries = query_rows.reshape(images, PATCHES, heads_dev, HS)
    keys = key_rows.reshape(images, PATCHES, heads_dev, HS)
    values = value_rows.reshape(images, PATCHES, heads_dev, HS)
    scores = jnp.einsum("bqhe,bkhe->bhqk", queries, keys, preferred_element_type=jnp.float32) * (
        2.0 / math.sqrt(HS)
    )
    expo = jnp.exp(scores)
    probs = (expo / jnp.sum(expo, axis=-1, keepdims=True)).astype(jnp.bfloat16)
    attended = jnp.einsum("bhqk,bkhe->bqhe", probs, values, preferred_element_type=jnp.float32)
    attended = attended.astype(jnp.bfloat16).reshape(tok_count, width_hid)
    term = jnp.dot(attended, w_out, preferred_element_type=jnp.float32) + jnp.dot(
        hidden, w_down, preferred_element_type=jnp.float32
    )
    mixed = lax.psum(term, "hid")
    return (own_cols + mixed).astype(jnp.bfloat16)


def solution(mesh):
    in_specs = (
        P("chan", None, None),
        P("chan", None, "hid"),
        P("chan", "hid"),
        P("chan", "hid"),
        P("chan", "hid"),
        P("chan"),
        P("chan"),
        P("chan", None, "hid"),
        P("chan", "hid"),
        P("hid"),
        P("hid", "chan"),
        P("hid", "chan"),
    )
    out_specs = P(None, "chan")
    return jax.shard_map(
        on_device, mesh=mesh, in_specs=in_specs, out_specs=out_specs, check_vma=False
    )
```

profile of v0, /device:TPU:0, one launch (start us, length us, event | category | flops | bytes accessed | tf_op | source)
XLA Modules:
  0.0 780.2 jit_solution(2045412981143405703)
XLA Ops:
  6.5 0.8 broadcast_subtract_fusion
  7.3 0.6 copy-done.5
  7.9 1.0 fusion.40
  8.9 1.0 reshape.112
  10.0 0.2 multiply_reduce_fusion.1
  10.2 0.1 copy.58
  10.2 0.6 sqrt.7
  10.8 0.9 convert_element_type.64
  11.8 171.0 %fusion.1 = f32[96,256,768]{2,1,0:T(8,128)} fusion(f32[96,768]{1,0:T(8,128)S(1)} %convert_element_type.64, bf16[96,256,256]{2,1,0:T(8,128)(2,1)} %param.12, bf16[96,256,768]{2,1,0:T(8,128)(2,1)} %param.13), kind=kOutput, calls=%fused_computation.2 | convolution fusion | flops 10890510336 | bytes 126124032 | tf_op jit(solution)/shard_map/ctp,cpd->ctd/dot_general | solution.py:55
  182.8 72.9 %copy.57 = f32[96,256,768]{1,2,0:T(8,128)} copy(f32[96,256,768]{2,1,0:T(8,128)} %fusion.1) | data formatting | bytes 150994944 | tf_op jit(solution)/shard_map/mul | solution.py:57
  255.7 23.3 %multiply_reduce_fusion = f32[96,256,6]{1,2,0:T(8,128)S(1)} fusion(f32[96,256,6,128]{1,3,2,0:T(8,128)} %bitcast.4), kind=kLoop, calls=%fused_computation.5 | loop fusion | flops 37601280 | bytes 76087296 | tf_op jit(solution)/shard_map/reduce_sum | solution.py:14
  279.0 0.1 add_rsqrt_fusion
  279.1 43.4 %fusion.2 = f32[96,6,1,256]{3,2,1,0:T(1,128)S(1)} fusion(f32[96,6,128,1]{2,3,1,0:T(1,128)S(1)} %copy-done.1, f32[96,256,6,128]{1,3,2,0:T(8,128)} %bitcast.4, f32[96,256,6]{1,2,0:T(8,128)S(1)} %add_rsqrt_fusion), kind=kOutput, calls=%fused_computation.3 | convolution fusion | flops 245366784 | bytes 76972032 | tf_op jit(solution)/shard_map/cthe,che->cth/dot_general | solution.py:66
  322.5 0.2 fusion.35
  322.7 0.3 fusion.42
  323.0 0.4 copy.59
  323.4 48.9 %broadcast_multiply_fusion = f32[96,256,6,128]{1,3,2,0:T(8,128)} fusion(f32[96,256,6,128]{1,3,2,0:T(8,128)} %bitcast.4, f32[96,256,6]{1,2,0:T(8,128)S(1)} %copy.59), kind=kLoop, calls=%fused_computation.21 | loop fusion | flops 18874368 | bytes 151584768 | tf_op jit(solution)/shard_map/mul | solution.py:72
  372.3 74.2 %copy.60 = f32[96,256,6,128]{3,0,2,1:T(8,128)} copy(f32[96,256,6,128]{1,3,2,0:T(8,128)} %broadcast_multiply_fusion) | data formatting | bytes 150994944 | tf_op jit(solution)/shard_map/mul | solution.py:72
  446.4 0.4 copy.61
  446.9 34.5 %broadcast_divide_fusion = f32[12,256,6,128]{3,0,2,1:T(8,128)} fusion(f32[12,256,6]{0,2,1:T(8,128)S(1)} %copy.61, f32[96,256,6,128]{3,0,2,1:T(8,128)} %copy.60, s32[96]{0:T(128)} %copy-done.5), kind=kOutput, calls=%fused_computation.28 | convolution fusion | flops 2720269312 | bytes 85008768 | tf_op jit(solution)/shard_map/kc,cthe->kthe/dot_general | solution.py:71
  481.4 12.1 %copy.86 = f32[12,256,6,128]{1,3,2,0:T(8,128)} copy(f32[12,256,6,128]{3,0,2,1:T(8,128)} %broadcast_divide_fusion) | data formatting | bytes 18874368
  493.5 5.0 fusion.12
  498.5 0.9 copy.82
  499.4 0.0 all-reduce.3.cloned.1.call-update
  499.5 0.0 all-gather.4.cloned.1.call-start
  499.5 47.0 %all-reduce.3.cloned.1.call-done = bf16[256,768]{1,0:T(8,128)(2,1)} async-done(((bf16[256,768]{1,0:T(8,128)(2,1)}), bf16[256,768]{1,0:T(8,128)(2,1)}) %all-reduce.3.cloned.1.call-update) | async-done | bytes 393232 | tf_op jit(solution)/shard_map/psum | solution.py:79
  546.5 0.0 reduce-scatter.5.cloned.1.call-start
  546.5 39.8 %all-gather.4.cloned.1.call-done = bf16[256,6144]{1,0:T(8,128)(2,1)} async-done(((bf16[256,768]{1,0:T(8,128)(2,1)}), bf16[256,6144]{1,0:T(8,128)(2,1)}) %all-gather.4.cloned.1.call-update) | async-done | bytes 3145744 | tf_op jit(solution)/shard_map/all_gather | solution.py:80
  586.3 3.2 convert_reduce_fusion
  589.5 7.8 %convolution_convert_fusion = bf16[256,3072]{1,0:T(8,128)(2,1)} fusion(bf16[1536,3072]{1,0:T(8,128)(2,1)} %param.20, f32[1536]{0:T(1024)S(1)} %copy-done.7, f32[256]{0:T(256)S(1)} %get-tuple-element.12, f32[256]{0:T(256)S(1)} %get-tuple-element.11, bf16[256,6144]{1,0:T(8,128)(2,1)} %all-gather.4.cloned.1.call-done, s32[]{:T(128)S(6)} %select_n.3), kind=kOutput, calls=%fused_computation.29 | convolution fusion | flops 2418671616 | bytes 11804676 | tf_op jit(solution)/shard_map/dot_general | solution.py:92
  597.4 0.0 reduce-scatter.5.cloned.1.call-update
  597.4 0.0 reduce-scatter.3.cloned.1.call-start
  597.4 6.5 convolution_convert_fusion.1
  603.9 0.3 all-gather.6.cloned.1.call-start
  604.2 23.3 %reduce-scatter.5.cloned.1.call-done = bf16[64,3072]{1,0:T(8,128)(2,1)} async-done(((bf16[256,3072]{1,0:T(8,128)(2,1)}), bf16[64,3072]{1,0:T(8,128)(2,1)}) %reduce-scatter.5.cloned.1.call-update) | async-done | bytes 393232 | tf_op jit(solution)/shard_map/reduce_scatter | solution.py:97
  627.6 3.5 fusion.20
  631.1 0.0 all-reduce.5.cloned.1.call-start
  631.1 28.0 %reduce-scatter.3.cloned.1.call-done = bf16[64,3,768]{2,0,1:T(8,128)(2,1)} async-done(((bf16[256,3,768]{2,0,1:T(8,128)(2,1)}), bf16[64,3,768]{2,0,1:T(8,128)(2,1)}) %reduce-scatter.3.cloned.1.call-update) | async-done | bytes 294928 | tf_op jit(solution)/shard_map/reduce_scatter | solution.py:94
  659.1 0.9 slice.13
  660.0 9.5 %all-gather = bf16[256,1,768]{2,0,1:T(8,128)(2,1)S(1)} all-gather(bf16[64,1,768]{2,0,1:T(8,128)(2,1)S(1)} %slice.13), channel_id=2, replica_groups=mesh['chan'=4,'hid'=8] {'chan'}, dimensions={0}, use_global_device_ids=true | all-gather | bytes 491520 | tf_op jit(solution)/shard_map/all_gather | solution.py:107
  669.6 0.9 copy.63
  670.5 1.0 convert_element_type.72
  671.5 0.7 slice_multiply_fusion
  672.2 1.0 mul.158
  673.2 0.1 reduce_sum.68
  673.3 0.1 copy.67
  673.4 0.1 copy.68
  673.5 0.1 reduce_sum.67
  673.7 0.1 copy.64
  673.8 0.1 copy.65
  673.9 0.1 mul.159
  674.0 0.1 mul.154
  674.1 0.7 fusion.36
  674.9 10.6 %all_gather.18 = bf16[256,768]{1,0:T(8,128)(2,1)S(1)} all-gather(bf16[64,768]{1,0:T(8,128)(2,1)S(1)} %get-tuple-element.7), channel_id=1, replica_groups=mesh['chan'=4,'hid'=8] {'chan'}, dimensions={0}, use_global_device_ids=true | all-gather | bytes 491520 | tf_op jit(solution)/shard_map/all_gather | solution.py:106
  685.4 0.2 copy.69
  685.6 11.0 %all_gather.17 = bf16[256,768]{1,0:T(8,128)(2,1)S(1)} all-gather(bf16[64,768]{1,0:T(8,128)(2,1)} %get-tuple-element.8), channel_id=1, replica_groups=mesh['chan'=4,'hid'=8] {'chan'}, dimensions={0}, use_global_device_ids=true | all-gather | bytes 491520 | tf_op jit(solution)/shard_map/all_gather | solution.py:105
  696.6 0.2 copy.66
  696.8 1.6 multiply_exponential_fusion
  698.4 2.4 convolution_convert_fusion.2
  700.8 0.0 all-gather.6.cloned.1.call-done
  700.8 5.7 fusion.50
  706.5 2.0 convolution_add_fusion
  708.5 62.2 %all-reduce.5.cloned.1.call-done = f32[256,1536]{1,0:T(8,128)} async-done(((f32[256,1536]{1,0:T(8,128)}), f32[256,1536]{1,0:T(8,128)}) %all-reduce.5.cloned.1.call-update) | async-done | bytes 1572880 | tf_op jit(solution)/shard_map/psum | solution.py:124
  770.6 2.7 fusion.17
  (26 shorter events, 0.2 us)
Async XLA Ops:
  6.5 699.9 %copy-start = (bf16[768,1536]{1,0:T(8,128)(2,1)S(1)}, bf16[768,1536]{1,0:T(8,128)(2,1)}, u32[]{:S(2)}) copy-start(bf16[768,1536]{1,0:T(8,128)(2,1)} %param.22) | copy-start | bytes 7077892
  6.5 539.9 %all-reduce.3.cloned.1.call-start = ((), (), s32[]{:S(2)}) async-start(), calls=%async_computation.2 | async-start | bytes 786432 | tf_op jit(solution)/shard_map/psum | solution.py:79
  7.3 0.6 copy-start.5
  255.7 23.4 %copy-start.1 = (f32[96,6,128,1]{2,3,1,0:T(1,128)S(1)}, f32[96,6,128,1]{2,3,1,0:T(1,128)}, u32[]{:S(2)}) copy-start(f32[96,6,128,1]{2,3,1,0:T(1,128)} %reshape.112) | copy-start | bytes 884740
  255.7 66.8 %copy-start.3 = (f32[96,6]{0,1:T(8,128)S(1)}, f32[96,6]{0,1:T(8,128)}, u32[]{:S(2)}) copy-start(f32[96,6]{0,1:T(8,128)} %sqrt.7) | copy-start | bytes 6916
  255.7 67.0 %copy-start.6 = (s32[96]{0:T(128)S(1)}, s32[96]{0:T(128)}, u32[]{:S(2)}) copy-start(s32[96]{0:T(128)} %copy-done.5) | copy-start | bytes 1156
  279.0 44.4 %copy-start.2 = (bf16[12,768]{1,0:T(8,128)(2,1)S(1)}, bf16[12,768]{1,0:T(8,128)(2,1)}, u32[]{:S(2)}) copy-start(bf16[12,768]{1,0:T(8,128)(2,1)} %param.16) | copy-start | bytes 55300
  446.9 142.7 %copy-start.7 = (f32[1536]{0:T(1024)S(1)}, f32[1536]{0:T(1024)}, u32[]{:S(2)}) copy-start(f32[1536]{0:T(1024)} %param.18) | copy-start | bytes 18436
  446.9 180.7 %copy-start.4 = (f32[3072]{0:T(1024)S(1)}, f32[3072]{0:T(1024)}, u32[]{:S(2)}) copy-start(f32[3072]{0:T(1024)} %param.21) | copy-start | bytes 36868
  499.5 86.9 %all-gather.4.cloned.1.call-start = ((), (), s32[]{:S(2)}) async-start(), calls=%async_computation.3 | async-start | bytes 3538944 | tf_op jit(solution)/shard_map/all_gather | solution.py:80
  546.5 81.1 %reduce-scatter.5.cloned.1.call-start = ((), (), s32[]{:S(2)}) async-start(), calls=%async_computation.5 | async-start | bytes 1966080 | tf_op jit(solution)/shard_map/reduce_scatter | solution.py:97
  597.4 61.7 %reduce-scatter.3.cloned.1.call-start = ((), (), s32[]{:S(2)}) async-start(), calls=%async_computation.4 | async-start | bytes 1474560 | tf_op jit(solution)/shard_map/reduce_scatter | solution.py:94
  603.9 96.9 %all-gather.6.cloned.1.call-start = ((), (), s32[]{:S(2)}) async-start(), calls=%async_computation.6 | async-start | bytes 1966080 | tf_op jit(solution)/shard_map/all_gather | solution.py:108
  631.1 139.6 %all-reduce.5.cloned.1.call-start = ((), (), s32[]{:S(2)}) async-start(), calls=%async_computation.7 | async-start | bytes 3145728 | tf_op jit(solution)/shard_map/psum | solution.py:124
Sparse Core Ops, SparseCore 0:
  499.6 46.8 all-reduce.2
  548.1 38.1 all-gather.3
  597.5 30.0 reduce-scatter.4
  630.3 28.7 reduce-scatter.2
  660.8 33.7 all-gather.5
  708.6 61.9 all-reduce.4
where the time goes:
time: 783 us; the launch traced here: 780 us
  matrix products  276 us (35%)
  waiting for transfers between devices  200 us (26%)
  local copies, waits for them, and re-layouts  167 us (21%)
  other arithmetic  91.4 us (12%)
  blocking collectives  31.1 us (4%)
  between operations  13.7 us (2%)
    dot_general x1, matrix products, on_device(): jnp.einsum('ctp,cpd->ctd', pixels, patch_weight, preferred_element_type=j...  171 us
    mul x1, local copies, waits for them, and re-layouts, on_device(): weight[..., None] * split  74.2 us
    mul x1, local copies, waits for them, and re-layouts, on_device(): features = jax.nn.gelu(embedded, approximate=False)  72.9 us
    psum x1, waiting for transfers between devices, on_device(): mixed = lax.psum(term, 'hid')  62.2 us
    mul x1, other arithmetic, on_device(): weight[..., None] * split  48.9 us
    psum x1, waiting for transfers between devices, on_device(): layer_sum = lax.psum(partial_value.astype(jnp.bfloat16), 'chan')  47 us
    dot_general x1, matrix products, on_device(): jnp.einsum('cthe,che->cth', normed, query, precision=lax.Precision.HIGHEST)  43.4 us
    all_gather x1, waiting for transfers between devices, on_device(): gathered = lax.all_gather(layer_sum, 'hid', axis=1, tiled=True)  39.8 us
  transfers between devices with their start and end apart: 6, of which 5 were waited for; matrix products, arithmetic and copies ran while one was open for 3% of the time, Pallas kernels for 0%

commit v1 on v0

--- a/solution.py
+++ b/solution.py
@@ -121,7 +121,12 @@
     term = jnp.dot(attended, w_out, preferred_element_type=jnp.float32) + jnp.dot(
         hidden, w_down, preferred_element_type=jnp.float32
     )
-    mixed = lax.psum(term, "hid")
+
+    def draw_figure_now(x_in):
+        placed = lax.all_gather(x_in, axis_name="hid")
+        return jnp.sum(placed, axis=0)
+
+    mixed = draw_figure_now(term)
     return (own_cols + mixed).astype(jnp.bfloat16)
 
 

time: 783 us -> 845 us (1.079)
  waiting for transfers between devices: 200 us -> 255 us
    all_gather x0 -> x1, waiting for transfers between devices: none -> 117 us  [draw_figure_now(): placed = lax.all_gather(x_in, axis_name='hid')]
    psum x1 -> x0, waiting for transfers between devices: 62.2 us -> none  [on_device(): mixed = lax.psum(term, 'hid')]
  transfers between devices with their start and end apart: 6 -> 6, of which waited for: 5 -> 5; matrix products, arithmetic and copies ran while one was open for 3% -> 2% of each run, Pallas kernels for 0% -> 0%
where the time goes in v1:
time: 845 us; the launch traced here: 842 us
  matrix products  276 us (33%)
  waiting for transfers between devices  255 us (30%)
  local copies, waits for them, and re-layouts  167 us (20%)
  other arithmetic  98.7 us (12%)
  blocking collectives  31.1 us (4%)
  between operations  13.7 us (2%)
    dot_general x1, matrix products, on_device(): jnp.einsum('ctp,cpd->ctd', pixels, patch_weight, preferred_element_type=j...  171 us
    all_gather x1, waiting for transfers between devices, draw_figure_now(): placed = lax.all_gather(x_in, axis_name='hid')  117 us
    mul x1, local copies, waits for them, and re-layouts, on_device(): weight[..., None] * split  74.2 us
    mul x1, local copies, waits for them, and re-layouts, on_device(): features = jax.nn.gelu(embedded, approximate=False)  72.9 us
    mul x1, other arithmetic, on_device(): weight[..., None] * split  48.9 us
    psum x1, waiting for transfers between devices, on_device(): layer_sum = lax.psum(partial_value.astype(jnp.bfloat16), 'chan')  47 us
    dot_general x1, matrix products, on_device(): jnp.einsum('cthe,che->cth', normed, query, precision=lax.Precision.HIGHEST)  43.4 us
    all_gather x1, waiting for transfers between devices, on_device(): gathered = lax.all_gather(layer_sum, 'hid', axis=1, tiled=True)  39.8 us
  transfers between devices with their start and end apart: 6, of which 5 were waited for; matrix products, arithmetic and copies ran while one was open for 2% of the time, Pallas kernels for 0%

profile of v1, /device:TPU:0, one launch (start us, length us, event | category | flops | bytes accessed | tf_op | source)
XLA Modules:
  0.0 842.1 jit_solution(14783937349802541783)
XLA Ops:
  6.5 0.8 broadcast_subtract_fusion
  7.3 0.6 copy-done.5
  7.9 1.0 fusion.40
  8.9 1.0 reshape.113
  10.0 0.2 multiply_reduce_fusion.1
  10.2 0.1 copy.58
  10.2 0.6 sqrt.7
  10.8 0.9 convert_element_type.64
  11.8 171.0 %fusion.1 = f32[96,256,768]{2,1,0:T(8,128)} fusion(f32[96,768]{1,0:T(8,128)S(1)} %convert_element_type.64, bf16[96,256,256]{2,1,0:T(8,128)(2,1)} %param.12, bf16[96,256,768]{2,1,0:T(8,128)(2,1)} %param.13), kind=kOutput, calls=%fused_computation.2 | convolution fusion | flops 10890510336 | bytes 126124032 | tf_op jit(solution)/shard_map/ctp,cpd->ctd/dot_general | solution.py:55
  182.8 72.9 %copy.57 = f32[96,256,768]{1,2,0:T(8,128)} copy(f32[96,256,768]{2,1,0:T(8,128)} %fusion.1) | data formatting | bytes 150994944 | tf_op jit(solution)/shard_map/mul | solution.py:57
  255.7 23.3 %multiply_reduce_fusion = f32[96,256,6]{1,2,0:T(8,128)S(1)} fusion(f32[96,256,6,128]{1,3,2,0:T(8,128)} %bitcast.4), kind=kLoop, calls=%fused_computation.5 | loop fusion | flops 37601280 | bytes 76087296 | tf_op jit(solution)/shard_map/reduce_sum | solution.py:14
  279.0 0.1 add_rsqrt_fusion
  279.1 43.4 %fusion.2 = f32[96,6,1,256]{3,2,1,0:T(1,128)S(1)} fusion(f32[96,6,128,1]{2,3,1,0:T(1,128)S(1)} %copy-done.1, f32[96,256,6,128]{1,3,2,0:T(8,128)} %bitcast.4, f32[96,256,6]{1,2,0:T(8,128)S(1)} %add_rsqrt_fusion), kind=kOutput, calls=%fused_computation.3 | convolution fusion | flops 245366784 | bytes 76972032 | tf_op jit(solution)/shard_map/cthe,che->cth/dot_general | solution.py:66
  322.5 0.2 fusion.35
  322.7 0.3 fusion.42
  323.0 0.4 copy.59
  323.4 48.9 %broadcast_multiply_fusion = f32[96,256,6,128]{1,3,2,0:T(8,128)} fusion(f32[96,256,6,128]{1,3,2,0:T(8,128)} %bitcast.4, f32[96,256,6]{1,2,0:T(8,128)S(1)} %copy.59), kind=kLoop, calls=%fused_computation.21 | loop fusion | flops 18874368 | bytes 151584768 | tf_op jit(solution)/shard_map/mul | solution.py:72
  372.3 74.2 %copy.60 = f32[96,256,6,128]{3,0,2,1:T(8,128)} copy(f32[96,256,6,128]{1,3,2,0:T(8,128)} %broadcast_multiply_fusion) | data formatting | bytes 150994944 | tf_op jit(solution)/shard_map/mul | solution.py:72
  446.4 0.4 copy.61
  446.9 34.5 %broadcast_divide_fusion = f32[12,256,6,128]{3,0,2,1:T(8,128)} fusion(f32[12,256,6]{0,2,1:T(8,128)S(1)} %copy.61, f32[96,256,6,128]{3,0,2,1:T(8,128)} %copy.60, s32[96]{0:T(128)} %copy-done.5), kind=kOutput, calls=%fused_computation.28 | convolution fusion | flops 2720269312 | bytes 85008768 | tf_op jit(solution)/shard_map/kc,cthe->kthe/dot_general | solution.py:71
  481.4 12.1 %copy.86 = f32[12,256,6,128]{1,3,2,0:T(8,128)} copy(f32[12,256,6,128]{3,0,2,1:T(8,128)} %broadcast_divide_fusion) | data formatting | bytes 18874368
  493.5 5.0 fusion.12
  498.5 0.9 copy.82
  499.4 0.0 all-reduce.2.cloned.1.call-update
  499.5 0.0 all-gather.6.cloned.1.call-start
  499.5 47.0 %all-reduce.2.cloned.1.call-done = bf16[256,768]{1,0:T(8,128)(2,1)} async-done(((bf16[256,768]{1,0:T(8,128)(2,1)}), bf16[256,768]{1,0:T(8,128)(2,1)}) %all-reduce.2.cloned.1.call-update) | async-done | bytes 393232 | tf_op jit(solution)/shard_map/psum | solution.py:79
  546.5 0.0 reduce-scatter.5.cloned.1.call-start
  546.5 39.8 %all-gather.6.cloned.1.call-done = bf16[256,6144]{1,0:T(8,128)(2,1)} async-done(((bf16[256,768]{1,0:T(8,128)(2,1)}), bf16[256,6144]{1,0:T(8,128)(2,1)}) %all-gather.6.cloned.1.call-update) | async-done | bytes 3145744 | tf_op jit(solution)/shard_map/all_gather | solution.py:80
  586.3 3.2 convert_reduce_fusion
  589.5 7.8 convolution_convert_fusion
  597.4 0.0 reduce-scatter.3.cloned.1.call-start
  597.4 6.4 convolution_convert_fusion.1
  603.9 0.3 all-gather.8.cloned.1.call-start
  604.2 23.4 %reduce-scatter.5.cloned.1.call-done = bf16[64,3072]{1,0:T(8,128)(2,1)} async-done(((bf16[256,3072]{1,0:T(8,128)(2,1)}), bf16[64,3072]{1,0:T(8,128)(2,1)}) %reduce-scatter.5.cloned.1.call-update) | async-done | bytes 393232 | tf_op jit(solution)/shard_map/reduce_scatter | solution.py:97
  627.6 3.5 fusion.20
  631.1 0.0 all-gather.10.cloned.1.call-start
  631.1 28.0 %reduce-scatter.3.cloned.1.call-done = bf16[64,3,768]{2,0,1:T(8,128)(2,1)} async-done(((bf16[256,3,768]{2,0,1:T(8,128)(2,1)}), bf16[64,3,768]{2,0,1:T(8,128)(2,1)}) %reduce-scatter.3.cloned.1.call-update) | async-done | bytes 294928 | tf_op jit(solution)/shard_map/reduce_scatter | solution.py:94
  659.1 0.9 slice.13
  660.0 9.5 %all-gather = bf16[256,1,768]{2,0,1:T(8,128)(2,1)S(1)} all-gather(bf16[64,1,768]{2,0,1:T(8,128)(2,1)S(1)} %slice.13), channel_id=2, replica_groups=mesh['chan'=4,'hid'=8] {'chan'}, dimensions={0}, use_global_device_ids=true | all-gather | bytes 491520 | tf_op jit(solution)/shard_map/all_gather | solution.py:107
  669.6 0.9 copy.63
  670.5 1.0 convert_element_type.72
  671.5 0.7 slice_multiply_fusion
  672.2 1.0 mul.158
  673.1 0.1 reduce_sum.77
  673.3 0.1 copy.67
  673.4 0.1 copy.68
  673.5 0.1 reduce_sum.76
  673.7 0.1 copy.64
  673.8 0.1 copy.65
  673.9 0.1 mul.159
  674.0 0.1 mul.154
  674.1 0.7 fusion.36
  674.8 10.4 %all_gather.24 = bf16[256,768]{1,0:T(8,128)(2,1)S(1)} all-gather(bf16[64,768]{1,0:T(8,128)(2,1)S(1)} %get-tuple-element.7), channel_id=1, replica_groups=mesh['chan'=4,'hid'=8] {'chan'}, dimensions={0}, use_global_device_ids=true | all-gather | bytes 491520 | tf_op jit(solution)/shard_map/all_gather | solution.py:106
  685.3 0.2 copy.69
  685.5 11.1 %all_gather.23 = bf16[256,768]{1,0:T(8,128)(2,1)S(1)} all-gather(bf16[64,768]{1,0:T(8,128)(2,1)} %get-tuple-element.8), channel_id=1, replica_groups=mesh['chan'=4,'hid'=8] {'chan'}, dimensions={0}, use_global_device_ids=true | all-gather | bytes 491520 | tf_op jit(solution)/shard_map/all_gather | solution.py:105
  696.5 0.2 copy.66
  696.7 1.6 multiply_exponential_fusion
  698.3 2.4 convolution_convert_fusion.2
  700.7 0.0 all-gather.8.cloned.1.call-done
  700.7 5.7 fusion.50
  706.4 1.9 convolution_add_fusion
  708.4 116.9 %all-gather.10.cloned.1.call-done = f32[2048,1536]{1,0:T(8,128)} async-done(((f32[256,1536]{1,0:T(8,128)}), f32[2048,1536]{1,0:T(8,128)}) %all-gather.10.cloned.1.call-update) | async-done | bytes 12582928 | tf_op jit(solution)/shard_map/all_gather | solution.py:126
  825.3 7.3 reduce_sum.79
  832.6 2.7 fusion.17
  (27 shorter events, 0.2 us)
Async XLA Ops:
  6.5 699.9 %copy-start = (bf16[768,1536]{1,0:T(8,128)(2,1)S(1)}, bf16[768,1536]{1,0:T(8,128)(2,1)}, u32[]{:S(2)}) copy-start(bf16[768,1536]{1,0:T(8,128)(2,1)} %param.22) | copy-start | bytes 7077892
  6.5 539.9 %all-reduce.2.cloned.1.call-start = ((), (), s32[]{:S(2)}) async-start(), calls=%async_computation.2 | async-start | bytes 786432 | tf_op jit(solution)/shard_map/psum | solution.py:79
  7.3 0.6 copy-start.5
  255.7 23.4 %copy-start.1 = (f32[96,6,128,1]{2,3,1,0:T(1,128)S(1)}, f32[96,6,128,1]{2,3,1,0:T(1,128)}, u32[]{:S(2)}) copy-start(f32[96,6,128,1]{2,3,1,0:T(1,128)} %reshape.113) | copy-start | bytes 884740
  255.7 66.8 %copy-start.3 = (f32[96,6]{0,1:T(8,128)S(1)}, f32[96,6]{0,1:T(8,128)}, u32[]{:S(2)}) copy-start(f32[96,6]{0,1:T(8,128)} %sqrt.7) | copy-start | bytes 6916
  255.7 67.0 %copy-start.6 = (s32[96]{0:T(128)S(1)}, s32[96]{0:T(128)}, u32[]{:S(2)}) copy-start(s32[96]{0:T(128)} %copy-done.5) | copy-start | bytes 1156
  279.0 44.4 %copy-start.2 = (bf16[12,768]{1,0:T(8,128)(2,1)S(1)}, bf16[12,768]{1,0:T(8,128)(2,1)}, u32[]{:S(2)}) copy-start(bf16[12,768]{1,0:T(8,128)(2,1)} %param.16) | copy-start | bytes 55300
  446.9 142.7 %copy-start.7 = (f32[1536]{0:T(1024)S(1)}, f32[1536]{0:T(1024)}, u32[]{:S(2)}) copy-start(f32[1536]{0:T(1024)} %param.18) | copy-start | bytes 18436
  446.9 180.7 %copy-start.4 = (f32[3072]{0:T(1024)S(1)}, f32[3072]{0:T(1024)}, u32[]{:S(2)}) copy-start(f32[3072]{0:T(1024)} %param.21) | copy-start | bytes 36868
  499.5 86.9 %all-gather.6.cloned.1.call-start = ((), (), s32[]{:S(2)}) async-start(), calls=%async_computation.3 | async-start | bytes 3538944 | tf_op jit(solution)/shard_map/all_gather | solution.py:80
  546.5 81.1 %reduce-scatter.5.cloned.1.call-start = ((), (), s32[]{:S(2)}) async-start(), calls=%async_computation.5 | async-start | bytes 1966080 | tf_op jit(solution)/shard_map/reduce_scatter | solution.py:97
  597.4 61.7 %reduce-scatter.3.cloned.1.call-start = ((), (), s32[]{:S(2)}) async-start(), calls=%async_computation.4 | async-start | bytes 1474560 | tf_op jit(solution)/shard_map/reduce_scatter | solution.py:94
  603.9 96.8 %all-gather.8.cloned.1.call-start = ((), (), s32[]{:S(2)}) async-start(), calls=%async_computation.6 | async-start | bytes 1966080 | tf_op jit(solution)/shard_map/all_gather | solution.py:108
  631.1 194.2 %all-gather.10.cloned.1.call-start = ((), (), s32[]{:S(2)}) async-start(), calls=%async_computation.7 | async-start | bytes 14155776 | tf_op jit(solution)/shard_map/all_gather | solution.py:126
Sparse Core Ops, SparseCore 0:
  499.6 46.8 all-reduce.1
  548.1 38.1 all-gather.5
  597.5 30.0 reduce-scatter.4
  630.4 28.7 reduce-scatter.2
  660.8 33.6 all-gather.7
  708.5 116.7 all-gather.9
